TPU v7x, 256 devices: a whole 4x4x8 slice. The times are simulated.
256 devices in a mesh: dp: 16 (over x, z_hi, core), ctx: 16 (over z_lo, y).
Axes of the slice: x: 4, y: 4, z: 8 (z_hi: 2, z_lo: 4; z = z_hi * 4 + z_lo), core: 2. Of those that a mesh axis runs over, the one named last changes fastest.
Arguments:
- tokens: bfloat16 [16, 4096, 2560], P('dp', 'ctx'), may hold values from -6 to 6
- w_x: bfloat16 [2560, 2560], P(None, 'dp'), may hold values from -0.125 to 0.125
- w_bc: bfloat16 [2560, 256], replicated, may hold values from -0.009765625 to 0.009765625
- w_dt: bfloat16 [2560, 40], replicated, may hold values from -0.125 to 0.125
- dt_bias: float32 [40], replicated, may hold values from -1 to 1
- decay_rate: float32 [40], replicated, may hold values from 0.00012207031 to 0.08
- skip_gain: float32 [40], replicated, may hold values from 0.5 to 1.5
- grad_y: bfloat16 [16, 4096, 2560], P('dp', 'ctx'), may hold values from -6 to 6
Outputs:
- head_out: bfloat16 [16, 4096, 2560], P('dp', 'ctx')
- d_tokens: bfloat16 [16, 4096, 2560], P('dp', 'ctx')
All inputs are finite; a program needn't handle non-finite values.
Results may differ from a plain program's by a relative error of at most 0.017.
Values may be sent and summed in bfloat16 or wider, within the bound.
A program may use at most 128 MiB of HBM per device.

v0:
```python
import jax
import jax.numpy as jnp
from jax import lax
from jax.sharding import PartitionSpec as P

Q = 256
HIGHEST_PRECISION = lax.Precision.HIGHEST


def prefix(value, axis, combine, identity, reverse):
    peers, mine = (lax.axis_size(axis), lax.axis_index(axis))
    everything = jax.tree.map(
        lambda part, kind: lax.all_gather(part.astype(kind), axis),
        value,
        (jnp.bfloat16, jnp.bfloat16),
    )
    start = jax.tree.map(
        lambda part, zero: jnp.broadcast_to(jnp.asarray(zero, part.dtype), part.shape),
        value,
        identity,
    )

    def lap(k, before):
        at = peers - 1 - k if reverse else k
        reached = at > mine if reverse else at < mine
        new = combine(
            before, jax.tree.map(lambda part, own: part[at].astype(own.dtype), everything, value)
        )
        return jax.tree.map(lambda a, b: jnp.where(reached, a, b), new, before)

    return lax.fori_loop(0, peers, lap, start)


def group_rates(raw_block, rate_vec, bias_vec):
    step_size = jax.nn.softplus(raw_block + bias_vec[None, :])
    running = jnp.cumsum(-rate_vec[None, :] * step_size, axis=0)
    return (step_size, running)


def group_forward(entering, pieces, rate_vec, bias_vec, skip_vec):
    x_block, raw_block, b_block, c_block = pieces
    step_size, running = group_rates(raw_block, rate_vec, bias_vec)
    length = x_block.shape[0]
    scores = jnp.dot(
        c_block.astype(jnp.bfloat16),
        b_block.astype(jnp.bfloat16).T,
        preferred_element_type=jnp.float32,
    )
    causal = jnp.arange(length)[:, None] >= jnp.arange(length)[None, :]
    by_head = running.T
    spread = by_head[:, :, None] - by_head[:, None, :]
    decays = jnp.exp(jnp.where(causal[None, :, :], spread, -1e30))
    mixing = scores[None, :, :] * decays * step_size.T[:, None, :]
    within = jnp.einsum("hij,jhp->ihp", mixing, x_block, precision=HIGHEST_PRECISION)
    carried = (
        jnp.einsum("in,hpn->ihp", c_block, entering, precision=HIGHEST_PRECISION)
        * jnp.exp(running)[:, :, None]
    )
    outputs = within + carried + skip_vec[None, :, None] * x_block
    weights_tail = jnp.exp(running[-1][None, :] - running) * step_size
    updated = jnp.exp(running[-1])[:, None, None] * entering + jnp.einsum(
        "jh,jhp,jn->hpn", weights_tail, x_block, b_block, precision=HIGHEST_PRECISION
    )
    return (updated, outputs)


def split_blocks(array, count):
    return array.reshape((count, array.shape[0] // count) + array.shape[1:])


def run_block(values, entering, rate_vec, bias_vec, skip_vec):
    x_all = values[0]
    count = x_all.shape[0] // Q

    def run_advance(carried_in, pieces):
        return group_forward(carried_in, pieces, rate_vec, bias_vec, skip_vec)

    final_state, outputs = lax.scan(
        run_advance, entering, tuple((split_blocks(member, count) for member in values))
    )
    return (outputs.reshape(x_all.shape), final_state)


def block_state(x_all, raw_all, b_all, rate_vec, bias_vec):
    count = x_all.shape[0] // Q

    def block_advance(entering, pieces):
        x_block, raw_block, b_block = pieces
        step_size, running = group_rates(raw_block, rate_vec, bias_vec)
        weights_tail = jnp.exp(running[-1][None, :] - running) * step_size
        updated = jnp.exp(running[-1])[:, None, None] * entering + jnp.einsum(
            "jh,jhp,jn->hpn", weights_tail, x_block, b_block, precision=HIGHEST_PRECISION
        )
        return (updated, running[-1])

    zero_state = jnp.zeros((x_all.shape[1], x_all.shape[2], b_all.shape[1]), jnp.float32)
    final_state, totals = lax.scan(
        block_advance,
        zero_state,
        (split_blocks(x_all, count), split_blocks(raw_all, count), split_blocks(b_all, count)),
    )
    return (jnp.exp(jnp.sum(totals, axis=0)), final_state)


def combine_states(earlier, later):
    return (earlier[0] * later[0], later[0][:, None, None] * earlier[1] + later[1])


def combine_grads(earlier, later):
    return (earlier[0] * later[0], later[1] + later[0][:, None, None] * earlier[1])


def local(tokens, w_x, w_bc, w_dt, dt_bias, decay_rate, skip_gain, grad_y):
    tok_rows = tokens[0]
    steps_here = tok_rows.shape[0]
    head_count = dt_bias.shape[0]
    width_hp = grad_y.shape[2]
    head_size = width_hp // head_count
    state_size = w_bc.shape[1] // 2
    contract = (((1,), (1,)), ((), ()))
    full_panel = lax.all_gather(w_x, "dp", axis=1, tiled=True)
    x_round = jnp.dot(tok_rows, full_panel, preferred_element_type=jnp.float32).astype(jnp.bfloat16)
    bc_round = jnp.dot(tok_rows, w_bc, preferred_element_type=jnp.float32).astype(jnp.bfloat16)
    raw_dt = jnp.dot(tok_rows, w_dt, preferred_element_type=jnp.float32)
    x_float = (
        lax.optimization_barrier(x_round)
        .astype(jnp.float32)
        .reshape(steps_here, head_count, head_size)
    )
    bc_float = lax.optimization_barrier(bc_round).astype(jnp.float32)
    b_float = bc_float[:, :state_size]
    c_float = bc_float[:, state_size:]
    grad_float = grad_y[0].astype(jnp.float32).reshape(steps_here, head_count, head_size)
    decay_total, local_state = block_state(x_float, raw_dt, b_float, decay_rate, dt_bias)
    step_size = jax.nn.softplus(raw_dt + dt_bias[None, :])
    running = jnp.cumsum(-decay_rate[None, :] * step_size, axis=0)
    direct_grad = jnp.einsum(
        "th,thp,tn->hpn", jnp.exp(running), grad_float, c_float, precision=HIGHEST_PRECISION
    )
    unit_decay = jnp.ones_like(decay_total)
    zero_state = jnp.zeros_like(local_state)
    entering = prefix(
        (decay_total, local_state), "ctx", combine_states, (unit_decay, zero_state), False
    )[1]
    later_grad = prefix(
        (decay_total, direct_grad), "ctx", combine_grads, (unit_decay, zero_state), True
    )[1]

    def forward(x_arg, raw_arg, b_arg, c_arg):
        return run_block((x_arg, raw_arg, b_arg, c_arg), entering, decay_rate, dt_bias, skip_gain)

    (head_float, final_state), backward = jax.vjp(forward, x_float, raw_dt, b_float, c_float)
    grad_x, grad_raw, grad_b, grad_c = backward((grad_float, later_grad))
    grad_x_round = grad_x.reshape(steps_here, width_hp).astype(jnp.bfloat16)
    grad_bc_round = jnp.concatenate([grad_b, grad_c], axis=1).astype(jnp.bfloat16)
    grad_raw_round = grad_raw.astype(jnp.bfloat16)
    total = lax.dot_general(grad_x_round, full_panel, contract, preferred_element_type=jnp.float32)
    total = total + lax.dot_general(
        grad_bc_round, w_bc, contract, preferred_element_type=jnp.float32
    )
    total = total + lax.dot_general(
        grad_raw_round, w_dt, contract, preferred_element_type=jnp.float32
    )
    head_out = head_float.reshape(steps_here, width_hp).astype(jnp.bfloat16)
    return (head_out[None], total.astype(jnp.bfloat16)[None])


def solution(mesh):
    placed = (P("dp", "ctx", None), P(None, "dp"), P(), P(), P(), P(), P(), P("dp", "ctx", None))
    return jax.shard_map(
        local,
        mesh=mesh,
        in_specs=placed,
        out_specs=(P("dp", "ctx", None), P("dp", "ctx", None)),
        check_vma=False,
    )
```

profile of v0, /device:TPU:1, one launch (start us, length us, event | category | flops | bytes accessed | tf_op | source)
XLA Modules:
  0.0 483.8 jit_solution(281639778616257343)
XLA Ops:
  10.9 1.8 fusion.51
  12.7 1.6 copy.35
  14.4 2.3 fusion.42
  17.7 39.7 %all-gather.2 = bf16[16,1,40]{2,1,0:T(2,128)(2,1)S(1)} all-gather(bf16[1,1,40]{2,1,0:T(2,128)(2,1)S(1)} %bitcast.230), channel_id=1, replica_groups=mesh['dp'=16,'ctx'=16] {'ctx'}, dimensions={0}, use_global_device_ids=true | all-gather | bytes 1360 | tf_op jit(solution)/shard_map/all_gather | solution.py:13
  57.6 86.7 %all-gather.11.cloned.1.call-done = bf16[640,64,128]{2,1,0:T(8,128)(2,1)} async-done(((bf16[40,64,128]{2,1,0:T(8,128)(2,1)}), bf16[640,64,128]{2,1,0:T(8,128)(2,1)}) %all-gather.11.cloned.1.call-update) | async-done | bytes 10485776 | tf_op jit(solution)/shard_map/all_gather | solution.py:13
  144.3 23.8 %while.23 = (s32[]{:T(128)}, f32[40,64,128]{2,1,0:T(8,128)S(1)}, s32[]{:T(128)}, bf16[16,40,64,128]{3,2,1,0:T(8,128)(2,1)}, bf16[16,40]{1,0:T(8,128)(2,1)S(1)}, ...) while((s32[]{:T(128)}, f32[40,64,128]{2,1,0:T(8,128)S(1)}, s32[]{:T(128)}, ...), condition=%wide.region_5.6_spmd.clone, body=%wide.region_4.5_spmd.clone.sunk | while | flops 1638448 | bytes 3277367 | solution.py:31
  145.7 1.4 fusion.134
  148.7 1.4 fusion.134
  154.6 1.4 fusion.134
  156.1 1.5 fusion.134
  157.6 1.6 fusion.134
  162.2 1.4 fusion.134
  166.6 1.4 fusion.134
  168.0 121.4 %all-gather.7.cloned.1.call-done = bf16[2560,2560]{0,1:T(8,128)(2,1)} async-done(((bf16[2560,160]{0,1:T(8,128)(2,1)}), bf16[2560,2560]{0,1:T(8,128)(2,1)}) %all-gather.7.cloned.1.call-update) | async-done | bytes 13107216 | tf_op jit(solution)/shard_map/all_gather | solution.py:121
  289.5 9.4 %convolution_convert_fusion = bf16[256,2560]{1,0:T(8,128)(2,1)} fusion(bf16[2560,2560]{0,1:T(8,128)(2,1)} %all-gather.7.cloned.1.call-done, bf16[1,256,2560]{2,1,0:T(8,128)(2,1)S(1)} %copy-done), kind=kOutput, calls=%fused_computation.39 | convolution fusion | flops 3356098560 | bytes 15728640 | tf_op jit(solution)/shard_map/dot_general | solution.py:122
  298.8 2.4 copy.34
  301.3 4.1 fusion.30
  305.6 2.3 fusion.41
  307.9 3.0 bitcast_multiply_fusion.2
  311.3 9.3 %fusion.10 = (f32[40,256]{1,0:T(8,128)}, f32[40,256]{1,0:T(8,128)}, f32[40,256]{1,0:T(8,128)}, bf16[256,256]{1,0:T(8,128)(2,1)S(1)}) fusion(f32[40,256]{1,0:T(8,128)S(1)} %get-tuple-element.612, f32[40,256]{1,0:T(8,128)S(1)} %get-tuple-element.610, f32[256,256]{1,0:T(8,128)S(1)} %fusion.76, pred[256,256]{1,0:T(8,128)(4,1)S(1)} %iota_compare_fusion, ...), kind=kOutput, calls=%fused_computation.17 | convolution fusion | flops 369526784 | bytes 3284992 | tf_op jit(solution)/shard_map/transpose(jvp())/while/body/eval_jaxpr/hij,jhp->ihp/dot_general | solution.py:54
  321.1 2.5 fusion.58
  323.7 7.3 %fusion.34 = bf16[256,40,64]{0,2,1:T(8,128)(2,1)S(1)} fusion(bf16[256,40,64]{0,2,1:T(8,128)(2,1)S(1)} %bitcast.214, f32[256,40,64]{0,2,1:T(8,128)S(1)} %copy-done.9, bf16[40,64,256]{2,1,0:T(8,128)(2,1)S(1)} %bitcast.215, f32[40,256]{1,0:T(8,128)S(1)} %copy-done.17, f32[40,256]{1,0:T(8,128)S(1)} %copy-done.15, f32[256,256]{1,0:T(8,128)S(1)} %fusion.76, ...), kind=kOutput, calls=%fused_computation.49 | convolution fusion | flops 2027683840 | bytes 7004320 | tf_op jit(solution)/shard_map/transpose(jvp())/while/body/eval_jaxpr/hij,jhp->ihp/dot_general | solution.py:54
  331.0 5.2 %fusion.111 = f32[256,2560]{1,0:T(8,128)} fusion(bf16[256,2560]{0,1:T(8,128)(2,1)S(1)} %bitcast.223, bf16[2560,2560]{0,1:T(8,128)(2,1)S(1)} %bitcast.211), kind=kOutput, calls=%fused_computation.148 | convolution fusion | flops 3355443200 | bytes 17039360 | tf_op jit(solution)/shard_map/dot_general | solution.py:157
  336.3 89.4 %all-gather.9.cloned.1.call-done = bf16[640,64,128]{2,1,0:T(8,128)(2,1)} async-done(((bf16[40,64,128]{2,1,0:T(8,128)(2,1)}), bf16[640,64,128]{2,1,0:T(8,128)(2,1)}) %all-gather.9.cloned.1.call-update) | async-done | bytes 10485776 | tf_op jit(solution)/shard_map/all_gather | solution.py:13
  425.7 23.3 %while.22 = (s32[]{:T(128)}, f32[40,64,128]{2,1,0:T(8,128)S(1)}, s32[]{:T(128)}, bf16[16,40]{1,0:T(8,128)(2,1)S(1)}, bf16[16,40,64,128]{3,2,1,0:T(8,128)(2,1)}, /*index=5*/s32[]{:T(128)}, s32[]{:T(128)}) while((s32[]{:T(128)}, f32[40,64,128]{2,1,0:T(8,128)S(1)}, s32[]{:T(128)}, bf16[16,40]{1,0:T(8,128)(2,1)S(1)}, ...), condition=%wide.region_3.4_spmd.clone, body=%wide.region_2.3_spmd.clone.sunk | while | flops 1638444 | bytes 3277305 | solution.py:31
  449.0 1.8 multiply_reduce_fusion.1
  450.8 2.8 fusion.35
  454.6 2.5 reduce-window.32
  457.3 10.9 %fusion.29 = bf16[256,40,64]{0,2,1:T(8,128)(2,1)} fusion(bf16[256,40,64]{0,2,1:T(8,128)(2,1)} %bitcast.219, f32[256,40,64]{0,2,1:T(8,128)} %get-tuple-element.617, f32[40,256]{1,0:T(8,128)} %copy-done.16, f32[40,256]{1,0:T(8,128)} %copy-done.14, f32[256,256]{1,0:T(8,128)S(1)} %fusion.76, pred[256,256]{1,0:T(8,128)(4,1)} %copy-done.12, ...), kind=kOutput, calls=%fused_computation.44 | convolution fusion | flops 2027683840 | bytes 5693600 | tf_op jit(solution)/shard_map/jvp()/while/body/eval_jaxpr/hij,jhp->ihp/dot_general | solution.py:54
  468.2 2.4 copy.41
  470.7 4.2 fusion.57
  475.6 1.6 fusion.25
  (141 shorter events, 43.6 us)
Async XLA Ops:
  7.2 1.3 copy-start
  7.2 137.1 %all-gather.11.cloned.1.call-start = ((), (), s32[]{:S(2)}) async-start(), calls=%async_computation.2 | async-start | bytes 11141120 | tf_op jit(solution)/shard_map/all_gather | solution.py:13
  10.0 301.2 %copy-start.16 = (f32[40,256]{1,0:T(8,128)}, f32[40,256]{1,0:T(8,128)S(1)}, u32[]{:S(2)}) copy-start(f32[40,256]{1,0:T(8,128)S(1)} %get-tuple-element.612) | copy-start | bytes 122884
  14.4 3.1 copy-start.3
  16.7 272.8 %all-gather.7.cloned.1.call-start = ((), (), s32[]{:S(2)}) async-start(), calls=%async_computation | async-start | bytes 13926400 | tf_op jit(solution)/shard_map/all_gather | solution.py:121
  17.4 408.3 %all-gather.9.cloned.1.call-start = ((), (), s32[]{:S(2)}) async-start(), calls=%async_computation.1 | async-start | bytes 11141120 | tf_op jit(solution)/shard_map/all_gather | solution.py:13
  17.6 293.7 %copy-start.14 = (f32[40,256]{1,0:T(8,128)}, f32[40,256]{1,0:T(8,128)S(1)}, u32[]{:S(2)}) copy-start(f32[40,256]{1,0:T(8,128)S(1)} %get-tuple-element.610) | copy-start | bytes 122884
  168.0 133.2 %copy-start.1 = (f32[40,64,128]{2,1,0:T(8,128)}, f32[40,64,128]{2,1,0:T(8,128)S(1)}, u32[]{:S(2)}) copy-start(f32[40,64,128]{2,1,0:T(8,128)S(1)} %get-tuple-element.540) | copy-start | bytes 3932164
  301.3 4.3 copy-start.6
  310.9 9.6 %copy-start.12 = (pred[256,256]{1,0:T(8,128)(4,1)}, pred[256,256]{1,0:T(8,128)(4,1)S(1)}, u32[]{:S(2)}) copy-start(pred[256,256]{1,0:T(8,128)(4,1)S(1)} %iota_compare_fusion) | copy-start | bytes 196612
  311.2 9.8 %copy-start.2 = (f32[40,64,128]{2,1,0:T(8,128)S(1)}, f32[40,64,128]{2,1,0:T(8,128)}, u32[]{:S(2)}) copy-start(f32[40,64,128]{2,1,0:T(8,128)} %copy-done.1) | copy-start | bytes 3932164
  311.2 9.8 %copy-start.7 = (bf16[256,2560]{0,1:T(8,128)(2,1)S(1)}, bf16[256,2560]{0,1:T(8,128)(2,1)}, u32[]{:S(2)}) copy-start(bf16[256,2560]{0,1:T(8,128)(2,1)} %copy.34) | copy-start | bytes 3932164
  311.2 12.4 %copy-start.9 = (f32[256,40,64]{0,2,1:T(8,128)S(1)}, f32[256,40,64]{0,2,1:T(8,128)}, u32[]{:S(2)}) copy-start(f32[256,40,64]{0,2,1:T(8,128)} %get-tuple-element.615) | copy-start | bytes 7864324
  311.2 19.7 %slice-start = ((s8[13107200]{0:T(1024)(128)(4,1)}), s8[4194304]{0:T(1024)(128)(4,1)S(1)}, s32[]{:S(2)}) async-start(s8[13107200]{0:T(1024)(128)(4,1)} %bitcast.210), calls=%async_computation.3 | async-start | bytes 8388608
  311.3 19.7 %slice-start.1 = ((s8[13107200]{0:T(1024)(128)(4,1)}), s8[4194304]{0:T(1024)(128)(4,1)S(1)}, s32[]{:S(2)}) async-start(s8[13107200]{0:T(1024)(128)(4,1)} %bitcast.210), calls=%async_computation.4 | async-start | bytes 8388608
  311.3 19.7 %slice-start.2 = ((s8[13107200]{0:T(1024)(128)(4,1)}), s8[4194304]{0:T(1024)(128)(4,1)S(1)}, s32[]{:S(2)}) async-start(s8[13107200]{0:T(1024)(128)(4,1)} %bitcast.210), calls=%async_computation.5 | async-start | bytes 8388608
  320.6 3.0 copy-start.4
  320.6 3.0 copy-start.15
  320.6 3.1 copy-start.17
  320.6 3.1 copy-start.19
  320.6 3.1 copy-start.13
  323.7 7.3 %slice-start.3 = ((s8[13107200]{0:T(1024)(128)(4,1)}), s8[524288]{0:T(1024)(128)(4,1)S(1)}, s32[]{:S(2)}) async-start(s8[13107200]{0:T(1024)(128)(4,1)} %bitcast.210), calls=%async_computation.6 | async-start | bytes 1048576
  449.0 1.8 copy-start.5
  470.7 4.3 copy-start.11
  470.7 4.3 copy-start.18
  470.7 4.9 %copy-start.8 = (f32[256,2560]{1,0:T(8,128)S(1)}, f32[256,2560]{1,0:T(8,128)}, u32[]{:S(2)}) copy-start(f32[256,2560]{1,0:T(8,128)} %fusion.111) | copy-start | bytes 7864324
  470.7 4.9 %copy-start.10 = (bf16[2560,256]{1,0:T(8,128)(2,1)S(1)}, bf16[2560,256]{1,0:T(8,128)(2,1)}, u32[]{:S(2)}) copy-start(bf16[2560,256]{1,0:T(8,128)(2,1)} %param.14) | copy-start | bytes 3932164
Sparse Core Ops, SparseCore 0:
  16.8 127.4 all-gather.10
  147.0 142.4 all-gather.6
  308.0 117.6 all-gather.8
where the time goes:
time: 486 us; the launch traced here: 484 us
  waiting for transfers between devices  298 us (61%)
  matrix products  66.4 us (14%)
  other arithmetic  56.4 us (12%)
  blocking collectives  39.7 us (8%)
  between operations  14.2 us (3%)
  local copies, waits for them, and re-layouts  7.68 us (2%)
    all_gather x2, waiting for transfers between devices, prefix(): lax.all_gather(part.astype(kind), axis)  176 us
    all_gather x1, waiting for transfers between devices, local(): full_panel = lax.all_gather(w_x, 'dp', axis=1, tiled=True)  121 us
    select_n x32, other arithmetic, lap(): return jax.tree.map(lambda a, b: jnp.where(reached, a, b), new, before)  45.6 us
    all_gather x1, blocking collectives, prefix(): lax.all_gather(part.astype(kind), axis)  39.7 us
    dot_general x3, matrix products, group_forward(): jnp.einsum('hij,jhp->ihp', mixing, x_block, precision=HIGHEST_PRECISION)  27.5 us
  transfers between devices with their start and end apart: 3, of which 3 were waited for; matrix products, arithmetic and copies ran while one was open for 11% of the time, Pallas kernels for 0%

commit v1 on v0

--- a/solution.py
+++ b/solution.py
@@ -118,7 +118,9 @@
     head_size = width_hp // head_count
     state_size = w_bc.shape[1] // 2
     contract = (((1,), (1,)), ((), ()))
-    full_panel = lax.all_gather(w_x, "dp", axis=1, tiled=True)
+    full_panel = jnp.concatenate(
+        lax.all_to_all(jnp.stack([w_x] * lax.axis_size("dp")), "dp", 0, 0), axis=1
+    )
     x_round = jnp.dot(tok_rows, full_panel, preferred_element_type=jnp.float32).astype(jnp.bfloat16)
     bc_round = jnp.dot(tok_rows, w_bc, preferred_element_type=jnp.float32).astype(jnp.bfloat16)
     raw_dt = jnp.dot(tok_rows, w_dt, preferred_element_type=jnp.float32)

time: 486 us -> 683 us (1.41)
  blocking collectives: 39.7 us -> 404 us
  waiting for transfers between devices: 298 us -> 103 us
  starting transfers between devices: 0.12 us -> 12.5 us
  local copies, waits for them, and re-layouts: 7.68 us -> 16.4 us
  other arithmetic: 56.4 us -> 64.6 us
    all_gather x1, blocking collectives: 39.7 us -> 404 us  [prefix(): lax.all_gather(part.astype(kind), axis)]
    all_gather x1 -> x0, waiting for transfers between devices: 121 us -> none  [local(): full_panel = lax.all_gather(w_x, 'dp', axis=1, tiled=True)]
    all_gather x2, waiting for transfers between devices: 176 us -> 103 us  [prefix(): lax.all_gather(part.astype(kind), axis)]
    all_to_all x0 -> x1, starting transfers between devices: none -> 12.4 us  [local(): lax.all_to_all(jnp.stack([w_x] * lax.axis_size('dp')), 'dp', 0, 0)]
    convert_element_type x32, other arithmetic: 0.34 us -> 10.7 us  [lap(): part[at].astype(own.dtype)]
    another operation x5 -> x6, local copies, waits for them, and re-layouts: 0.26 us -> 7.41 us  [the longest x1 7.15 us: local(): jnp.stack([w_x] * lax.axis_size('dp'))]
  transfers between devices with their start and end apart: 3 -> 3, of which waited for: 3 -> 1; matrix products, arithmetic and copies ran while one was open for 11% -> 9% of each run, Pallas kernels for 0% -> 0%
where the time goes in v1:
time: 683 us; the launch traced here: 681 us
  blocking collectives  404 us (59%)
  waiting for transfers between devices  103 us (15%)
  matrix products  65.1 us (10%)
  other arithmetic  64.6 us (9%)
  local copies, waits for them, and re-layouts  16.4 us (2%)
  between operations  14.7 us (2%)
  starting transfers between devices  12.5 us (2%)
    all_gather x1, blocking collectives, prefix(): lax.all_gather(part.astype(kind), axis)  404 us
    all_gather x2, waiting for transfers between devices, prefix(): lax.all_gather(part.astype(kind), axis)  103 us
    select_n x32, other arithmetic, lap(): return jax.tree.map(lambda a, b: jnp.where(reached, a, b), new, before)  45.7 us
    dot_general x3, matrix products, group_forward(): jnp.einsum('hij,jhp->ihp', mixing, x_block, precision=HIGHEST_PRECISION)  25.8 us
  transfers between devices with their start and end apart: 3, of which 1 were waited for; matrix products, arithmetic and copies ran while one was open for 9% of the time, Pallas kernels for 0%

profile of v1, /device:TPU:1, one launch (start us, length us, event | category | flops | bytes accessed | tf_op | source)
XLA Modules:
  0.0 680.9 jit_solution(4434538527779282627)
XLA Ops:
  7.3 1.7 copy.36
  11.1 1.8 fusion.51
  12.9 2.3 fusion.42
  15.2 7.2 %stack.2 = bf16[16,2560,160]{1,2,0:T(8,128)(2,1)} broadcast(bf16[2560,160]{0,1:T(8,128)(2,1)} %param.13), dimensions={1,2} | broadcast | bytes 13926400 | tf_op jit(solution)/shard_map/stack | solution.py:122
  22.4 12.4 %all-to-all-start = ((bf16[16,2560,160]{1,2,0:T(8,128)(2,1)}), bf16[16,2560,160]{1,2,0:T(8,128)(2,1)}, u32[]{:S(2)}, u32[]{:S(2)}) async-start(bf16[16,2560,160]{1,2,0:T(8,128)(2,1)} %stack.2), calls=%async_computation | async-start | bytes 26214400 | tf_op jit(solution)/shard_map/all_to_all | solution.py:122
  35.7 403.9 %all-gather.2 = bf16[16,1,40]{2,1,0:T(2,128)(2,1)S(1)} all-gather(bf16[1,1,40]{2,1,0:T(2,128)(2,1)S(1)} %bitcast.231), channel_id=1, replica_groups=mesh['dp'=16,'ctx'=16] {'ctx'}, dimensions={0}, use_global_device_ids=true | all-gather | bytes 1360 | tf_op jit(solution)/shard_map/all_gather | solution.py:13
  439.9 23.7 %while.23 = (s32[]{:T(128)}, f32[40,64,128]{2,1,0:T(8,128)S(1)}, s32[]{:T(128)}, bf16[16,40,64,128]{3,2,1,0:T(8,128)(2,1)}, bf16[16,40]{1,0:T(8,128)(2,1)S(1)}, ...) while((s32[]{:T(128)}, f32[40,64,128]{2,1,0:T(8,128)S(1)}, s32[]{:T(128)}, ...), condition=%wide.region_5.6_spmd.clone, body=%wide.region_4.5_spmd.clone.sunk | while | flops 1638448 | bytes 3277375 | solution.py:31
  439.9 1.4 fusion.134
  441.4 1.4 fusion.134
  442.9 1.4 fusion.134
  444.4 1.4 fusion.134
  447.3 1.4 fusion.134
  450.3 1.4 fusion.134
  454.7 1.4 fusion.134
  459.2 1.4 fusion.134
  463.6 9.8 %convolution_convert_fusion = bf16[256,2560]{1,0:T(8,128)(2,1)} fusion(bf16[2560,2560]{0,1:T(8,128)(2,1)} %bitcast.3, bf16[1,256,2560]{2,1,0:T(8,128)(2,1)S(1)} %copy-done), kind=kOutput, calls=%fused_computation.39 | convolution fusion | flops 3356098560 | bytes 15728640 | tf_op jit(solution)/shard_map/dot_general | solution.py:124
  473.4 1.6 copy.35
  476.1 2.7 fusion.30
  479.6 3.6 fusion.41
  483.2 1.7 bitcast_multiply_fusion.2
  485.9 10.0 %fusion.10 = (f32[40,256]{1,0:T(8,128)}, f32[40,256]{1,0:T(8,128)}, f32[40,256]{1,0:T(8,128)}, bf16[256,256]{1,0:T(8,128)(2,1)S(1)}) fusion(f32[40,256]{1,0:T(8,128)} %get-tuple-element.612, f32[40,256]{1,0:T(8,128)} %get-tuple-element.610, f32[256,256]{1,0:T(8,128)S(1)} %fusion.76, pred[256,256]{1,0:T(8,128)(4,1)S(1)} %iota_compare_fusion, ...), kind=kOutput, calls=%fused_computation.17 | convolution fusion | flops 369526784 | bytes 3284992 | tf_op jit(solution)/shard_map/transpose(jvp())/while/body/eval_jaxpr/hij,jhp->ihp/dot_general | solution.py:54
  496.4 2.5 fusion.58
  499.0 7.3 %fusion.34 = bf16[256,40,64]{0,2,1:T(8,128)(2,1)S(1)} fusion(bf16[256,40,64]{0,2,1:T(8,128)(2,1)S(1)} %bitcast.216, f32[256,40,64]{0,2,1:T(8,128)S(1)} %copy-done.12, bf16[40,64,256]{2,1,0:T(8,128)(2,1)S(1)} %bitcast.217, f32[40,256]{1,0:T(8,128)S(1)} %copy-done.28, f32[40,256]{1,0:T(8,128)S(1)} %copy-done.26, f32[256,256]{1,0:T(8,128)S(1)} %copy-done.16, ...), kind=kOutput, calls=%fused_computation.49 | convolution fusion | flops 2027683840 | bytes 7004320 | tf_op jit(solution)/shard_map/transpose(jvp())/while/body/eval_jaxpr/hij,jhp->ihp/dot_general | solution.py:54
  506.3 8.1 %fusion.111 = f32[256,2560]{1,0:T(8,128)} fusion(bf16[256,2560]{0,1:T(8,128)(2,1)S(1)} %bitcast.224, bf16[2560,2560]{0,1:T(8,128)(2,1)} %bitcast.3), kind=kOutput, calls=%fused_computation.148 | convolution fusion | flops 3355443200 | bytes 17039360 | tf_op jit(solution)/shard_map/dot_general | solution.py:159
  514.4 102.6 %all-gather.6.cloned.1.call-done = bf16[640,64,128]{2,1,0:T(8,128)(2,1)} async-done(((bf16[40,64,128]{2,1,0:T(8,128)(2,1)}), bf16[640,64,128]{2,1,0:T(8,128)(2,1)}) %all-gather.6.cloned.1.call-update) | async-done | bytes 10485776 | tf_op jit(solution)/shard_map/all_gather | solution.py:13
  617.1 33.6 %while.22 = (s32[]{:T(128)}, f32[40,64,128]{2,1,0:T(8,128)S(1)}, s32[]{:T(128)}, bf16[16,40]{1,0:T(8,128)(2,1)}, bf16[16,40,64,128]{3,2,1,0:T(8,128)(2,1)}, /*index=5*/s32[]{:T(128)}, s32[]{:T(128)}) while((s32[]{:T(128)}, f32[40,64,128]{2,1,0:T(8,128)S(1)}, s32[]{:T(128)}, bf16[16,40]{1,0:T(8,128)(2,1)}, ...), condition=%wide.region_3.4_spmd.clone, body=%wide.region_2.3_spmd.clone.sunk | while | flops 1638444 | bytes 3277313 | solution.py:31
  650.7 2.6 fusion.35
  654.6 8.6 %fusion.29 = bf16[256,40,64]{0,2,1:T(8,128)(2,1)S(1)} fusion(bf16[256,40,64]{0,2,1:T(8,128)(2,1)S(1)} %bitcast.222, f32[256,40,64]{0,2,1:T(8,128)S(1)} %get-tuple-element.617, f32[40,256]{1,0:T(8,128)S(1)} %copy-done.29, f32[40,256]{1,0:T(8,128)S(1)} %copy-done.27, f32[256,256]{1,0:T(8,128)S(1)} %copy-done.17, pred[256,256]{1,0:T(8,128)(4,1)S(1)} %copy-done.23, ...), kind=kOutput, calls=%fused_computation.44 | convolution fusion | flops 2027683840 | bytes 5693600 | tf_op jit(solution)/shard_map/jvp()/while/body/eval_jaxpr/hij,jhp->ihp/dot_general | solution.py:54
  663.3 1.6 copy.42
  665.2 2.8 reduce-window.32
  669.8 2.5 fusion.57
  672.4 1.7 fusion.25
  (176 shorter events, 54.9 us)
Async XLA Ops:
  7.2 432.6 %all-gather.8.cloned.1.call-start = ((), (), s32[]{:S(2)}) async-start(), calls=%async_computation.2 | async-start | bytes 11141120 | tf_op jit(solution)/shard_map/all_gather | solution.py:13
  9.0 6.2 copy-start.4
  11.0 467.8 %copy-start.31 = (f32[40,2]{0,1:T(2,128)}, f32[40,2]{0,1:T(2,128)S(1)}, u32[]{:S(2)}) copy-start(f32[40,2]{0,1:T(2,128)S(1)} %slice.47) | copy-start | bytes 964
  22.4 441.2 %all-to-all-start = ((bf16[16,2560,160]{1,2,0:T(8,128)(2,1)}), bf16[16,2560,160]{1,2,0:T(8,128)(2,1)}, u32[]{:S(2)}, u32[]{:S(2)}) async-start(bf16[16,2560,160]{1,2,0:T(8,128)(2,1)} %stack.2), calls=%async_computation | async-start | bytes 26214400 | tf_op jit(solution)/shard_map/all_to_all | solution.py:122
  34.8 582.3 %all-gather.6.cloned.1.call-start = ((), (), s32[]{:S(2)}) async-start(), calls=%async_computation.1 | async-start | bytes 11141120 | tf_op jit(solution)/shard_map/all_gather | solution.py:13
  439.8 38.9 %copy-start.33 = (f32[40]{0:T(128)}, f32[40]{0:T(128)S(1)}, u32[]{:S(2)}) copy-start(f32[40]{0:T(128)S(1)} %slice_reduce_fusion.2) | copy-start | bytes 484
  463.6 9.9 %copy-start.35 = (bf16[16,40]{1,0:T(8,128)(2,1)}, bf16[16,40]{1,0:T(8,128)(2,1)S(1)}, u32[]{:S(2)}) copy-start(bf16[16,40]{1,0:T(8,128)(2,1)S(1)} %get-tuple-element.738) | copy-start | bytes 3844
  463.6 11.5 %copy-start.2 = (f32[40,64,128]{2,1,0:T(8,128)}, f32[40,64,128]{2,1,0:T(8,128)S(1)}, u32[]{:S(2)}) copy-start(f32[40,64,128]{2,1,0:T(8,128)S(1)} %get-tuple-element.540) | copy-start | bytes 3932164
  478.8 4.4 copy-start.5
  479.6 5.4 copy-start.19
  485.0 10.9 %copy-start.22 = (pred[256,256]{1,0:T(8,128)(4,1)}, pred[256,256]{1,0:T(8,128)(4,1)S(1)}, u32[]{:S(2)}) copy-start(pred[256,256]{1,0:T(8,128)(4,1)S(1)} %iota_compare_fusion) | copy-start | bytes 196612
  485.2 10.7 %copy-start.15 = (f32[256,256]{1,0:T(8,128)}, f32[256,256]{1,0:T(8,128)S(1)}, u32[]{:S(2)}) copy-start(f32[256,256]{1,0:T(8,128)S(1)} %fusion.76) | copy-start | bytes 786436
  485.9 10.5 %copy-start.3 = (f32[40,64,128]{2,1,0:T(8,128)S(1)}, f32[40,64,128]{2,1,0:T(8,128)}, u32[]{:S(2)}) copy-start(f32[40,64,128]{2,1,0:T(8,128)} %copy-done.2) | copy-start | bytes 3932164
  485.9 10.5 %copy-start.8 = (bf16[256,2560]{0,1:T(8,128)(2,1)S(1)}, bf16[256,2560]{0,1:T(8,128)(2,1)}, u32[]{:S(2)}) copy-start(bf16[256,2560]{0,1:T(8,128)(2,1)} %copy-done.7) | copy-start | bytes 3932164
  485.9 10.5 %copy-start.20 = (f32[256,40]{0,1:T(8,128)S(1)}, f32[256,40]{0,1:T(8,128)}, u32[]{:S(2)}) copy-start(f32[256,40]{0,1:T(8,128)} %copy-done.19) | copy-start | bytes 122884
  485.9 13.0 %copy-start.12 = (f32[256,40,64]{0,2,1:T(8,128)S(1)}, f32[256,40,64]{0,2,1:T(8,128)}, u32[]{:S(2)}) copy-start(f32[256,40,64]{0,2,1:T(8,128)} %get-tuple-element.615) | copy-start | bytes 7864324
  495.9 3.1 copy-start.6
  495.9 3.1 copy-start.26
  495.9 3.1 copy-start.28
  495.9 3.1 copy-start.40
  495.9 3.1 copy-start.16
  495.9 3.1 copy-start.23
  663.2 1.8 copy-start.18
  663.2 1.8 copy-start.21
  663.2 1.8 copy-start.24
  663.2 1.8 copy-start.25
  663.2 4.8 copy-start.30
  663.2 4.8 copy-start.34
  663.3 4.8 copy-start.37
  668.7 3.6 copy-start.11
  668.7 3.6 copy-start.13
  669.8 4.2 copy-start.1
  (13 other events, 19.6 us)
Sparse Core Ops, SparseCore 0:
  15.3 271.8 all-gather.7
  483.3 133.7 all-gather.5
